TPU v7x, 128 devices: a whole 4x4x4 slice. The times are simulated.
128 devices in a mesh: pole: 2 (over y_lo), wave: 64 (over z, x, y_hi, core).
Axes of the slice: x: 4, y: 4 (y_hi: 2, y_lo: 2; y = y_hi * 2 + y_lo), z: 4, core: 2. Of those that a mesh axis runs over, the one named last changes fastest.
Arguments:
- tendency: bfloat16 [6, 2560, 128, 128], P('pole', 'wave'), may hold values from -6 to 6
- spectral_state: bfloat16 [6, 128, 128, 1280], P('pole', 'wave'), may hold values from -6 to 6
- legendre: bfloat16 [128, 1280, 2560], P('wave'), may hold values from -0.15625 to 0.15625
- gauss_weights: float32 [2560], P('wave'), may hold values from 0.35 to 1.05
- block_inverses: bfloat16 [64, 18, 128, 1280], P('pole', None, 'wave'), may hold values from -0.21875 to 0.21875
- pole_coeffs: float32 [64, 2], P('pole'), may hold values from -4 to 4
- wavenumbers: int32 [128], P('wave'), may hold values from 0 to 1279, as said below
Outputs:
- grid_state: bfloat16 [6, 2560, 128, 128], P('pole', 'wave')
Inputs may be any that keep to these rules, and one draw needn't show every extreme that they name: `wavenumbers`: entries 2 i and 2 i + 1 hold w and 1279 - w for some w below 640; all entries differ, and 0 is among them.
All inputs are finite; a program needn't handle non-finite values.
Results may differ from a plain program's by a relative error of at most 0.0062.
Values may be sent and summed in bfloat16 or wider, within the bound.
A program may use at most 128 MiB of HBM per device.

v0:
```python
import jax
import jax.numpy as jnp
from jax import lax
from jax.sharding import PartitionSpec as P


def mix_rows(real_matrix, imag_matrix, leading, trailing, orientation):
    summed = jnp.zeros(leading.shape, jnp.float32)
    for column in range(3):
        summed = summed + real_matrix[:, column, :, None, :] * leading[column][None]
        summed = summed + orientation * imag_matrix[:, column, :, None, :] * trailing[column][None]
    return summed


def per_device(
    tendency, spectral_state, legendre, gauss_weights, block_inverses, pole_coeffs, wavenumbers
):
    weighted = (tendency.astype(jnp.float32) * gauss_weights[None, :, None, None]).astype(
        jnp.bfloat16
    )
    received = lax.all_to_all(weighted, "wave", split_axis=2, concat_axis=1, tiled=True)
    spectral_tend = jnp.einsum(
        "rjse,snj->rsen", received, legendre, preferred_element_type=jnp.float32
    )
    degree = lax.broadcasted_iota(jnp.int32, (legendre.shape[0], legendre.shape[1]), 1)
    live_mask = (degree >= wavenumbers[:, None]).astype(jnp.float32)
    forced = (
        (spectral_state.astype(jnp.float32) + spectral_tend) * live_mask[None, :, None, :]
    ).astype(jnp.bfloat16)
    full_forced = lax.all_gather(forced, "pole", axis=0, tiled=True)
    pole_index = lax.axis_index("pole")
    local_pairs = block_inverses.shape[0]
    flat_inverse = block_inverses.reshape(local_pairs, -1).astype(jnp.float32)
    weighted_sums = jnp.dot(pole_coeffs.T, flat_inverse, precision=lax.Precision.HIGHEST)
    weighted_sums = weighted_sums.reshape(
        2, 2, 3, 3, block_inverses.shape[2], block_inverses.shape[3]
    )
    real_matrix = weighted_sums[0, 0] - weighted_sums[1, 1]
    imag_matrix = weighted_sums[0, 1] + weighted_sums[1, 0]
    forced_wide = full_forced.astype(jnp.float32)
    real_matrix, imag_matrix = lax.psum((real_matrix, imag_matrix), "pole")
    leading = lax.dynamic_slice_in_dim(forced_wide, pole_index * 3, 3, 0)
    trailing = lax.dynamic_slice_in_dim(forced_wide, (1 - pole_index) * 3, 3, 0)
    orientation = (2 * pole_index - 1).astype(jnp.float32)
    advanced_rows = mix_rows(real_matrix, imag_matrix, leading, trailing, orientation)
    advanced = advanced_rows.astype(jnp.bfloat16)
    synthesized = jnp.einsum(
        "rsen,snj->rjse", advanced, legendre, preferred_element_type=jnp.float32
    ).astype(jnp.bfloat16)
    return lax.all_to_all(synthesized, "wave", split_axis=1, concat_axis=2, tiled=True)


def solution(mesh):
    in_specs = (
        P("pole", "wave", None, None),
        P("pole", "wave", None, None),
        P("wave", None, None),
        P("wave"),
        P("pole", None, "wave", None),
        P("pole", None),
        P("wave"),
    )
    out_specs = P("pole", "wave", None, None)
    return jax.shard_map(
        per_device, mesh=mesh, in_specs=in_specs, out_specs=out_specs, check_vma=False
    )
```

profile of v0, /device:TPU:1, one launch (start us, length us, event | category | flops | bytes accessed | tf_op | source)
XLA Modules:
  0.0 246.0 jit_solution(9310441777758352411)
XLA Ops:
  6.5 0.0 copy-start
  6.5 6.6 %multiply_convert_fusion = bf16[3,40,128,128]{3,1,0,2:T(8,128)(2,1)} fusion(bf16[3,40,128,128]{3,2,1,0:T(8,128)(2,1)} %param.7, f32[40]{0:T(128)} %param.10), kind=kLoop, calls=%fused_computation.4 | loop fusion | flops 5898240 | bytes 7864480 | tf_op jit(solution)/shard_map/convert_element_type | solution.py:18
  13.1 0.0 copy-start.2
  13.1 12.9 %all-to-all-start = ((bf16[3,40,128,128]{3,1,0,2:T(8,128)(2,1)}), bf16[3,40,128,128]{3,1,0,2:T(8,128)(2,1)}, u32[]{:S(2)}, u32[]{:S(2)}) async-start(bf16[3,40,128,128]{3,1,0,2:T(8,128)(2,1)} %multiply_convert_fusion), calls=%async_computation | async-start | bytes 7864320 | tf_op jit(solution)/shard_map/all_to_all | solution.py:21
  26.0 0.0 all-reduce.3.cloned.1.call-start
  26.1 0.0 copy-done.2
  26.1 3.5 %reshape.54 = bf16[32,46080]{1,0:T(8,128)(2,1)} reshape(bf16[32,18,2,1280]{3,2,1,0:T(2,128)(2,1)S(1)} %copy-done.2) | data formatting | bytes 5898240 | tf_op jit(solution)/shard_map/reshape | solution.py:33
  29.6 0.0 copy-start.3
  29.6 4.0 %dot_general.14 = bf16[2,3,3,2,1280,32]{4,3,2,1,0,5:T(2,128)(2,1)S(1)} reshape(bf16[46080,32]{0,1:T(8,128)(2,1)} %bitcast.67) | data formatting | bytes 5898240 | tf_op jit(solution)/shard_map/dot_general | solution.py:34
  33.6 0.0 copy-done
  33.6 1.3 fusion.17
  34.9 0.2 slice_subtract_fusion
  35.1 0.8 copy_bitcast_fusion
  35.9 0.0 all-reduce.3.cloned.1.call-update
  35.9 0.2 all-gather.2.cloned.1.call-start
  36.1 0.0 copy-done.3
  36.1 0.1 compare_convert_fusion
  36.2 40.1 %all-to-all-done = bf16[3,40,128,128]{3,1,0,2:T(8,128)(2,1)} async-done(((bf16[3,40,128,128]{3,1,0,2:T(8,128)(2,1)}), bf16[3,40,128,128]{3,1,0,2:T(8,128)(2,1)}, u32[]{:S(2)}, u32[]{:S(2)}) %all-to-all-start) | async-done | bytes 3932192 | tf_op jit(solution)/shard_map/all_to_all | solution.py:21
  76.3 0.0 copy-start.4
  76.3 2.9 %copy.62 = bf16[3,64,40,2,128]{4,2,1,3,0:T(8,128)(2,1)S(1)} copy(bf16[3,64,40,2,128]{4,2,0,3,1:T(8,128)(2,1)} %bitcast.6) | data formatting | bytes 7864320 | tf_op jit(solution)/shard_map/all_to_all | solution.py:21
  79.2 0.0 copy-done.4
  79.2 10.4 %fusion.11 = bf16[3,2,128,1280]{3,2,0,1:T(8,128)(2,1)} fusion(bf16[2,1280,2560]{2,1,0:T(8,128)(2,1)} %param.9, bf16[3,2560,2,128]{3,1,2,0:T(8,128)(2,1)S(1)} %bitcast.68, bf16[3,2,128,1280]{3,2,1,0:T(8,128)(2,1)S(1)} %copy-done.4, f32[2,1280]{1,0:T(2,128)S(1)} %compare_convert_fusion), kind=kOutput, calls=%fused_computation.9 | convolution fusion | flops 5037096960 | bytes 20981760 | tf_op jit(solution)/shard_map/rjse,snj->rsen/dot_general | solution.py:22
  89.7 0.0 all-gather.2.cloned.1.call-update
  89.7 0.0 all-reduce.3.cloned.1.call-done
  89.7 0.8 fusion.33
  90.6 0.8 slice_bitcast_fusion.2
  91.5 56.5 %all-gather.2.cloned.1.call-done = bf16[6,2,128,1280]{3,2,0,1:T(8,128)(2,1)} async-done(((bf16[3,2,128,1280]{3,2,0,1:T(8,128)(2,1)}), bf16[6,2,128,1280]{3,2,0,1:T(8,128)(2,1)}) %all-gather.2.cloned.1.call-update) | async-done | bytes 3932176 | tf_op jit(solution)/shard_map/all_gather | solution.py:30
  148.0 2.9 %convert_element_type.40 = f32[6,2,128,1280]{3,2,0,1:T(8,128)S(1)} convert(bf16[6,2,128,1280]{3,2,0,1:T(8,128)(2,1)} %all-gather.2.cloned.1.call-done) | non-fusion elementwise | flops 1966080 | bytes 11796480 | tf_op jit(solution)/shard_map/convert_element_type | solution.py:40
  150.9 0.5 dynamic-slice_bitcast_fusion.5
  151.4 12.3 %fusion.7 = bf16[3,2560,2,128]{1,3,0,2:T(8,128)(2,1)} fusion(bf16[2,1280,2560]{2,1,0:T(8,128)(2,1)} %param.9, f32[2,128,1280]{2,1,0:T(8,128)S(1)} %get-tuple-element.11, f32[3,2,1280]{2,0,1:T(4,128)S(1)} %copy.68, f32[2,128,1280]{2,1,0:T(8,128)S(1)} %get-tuple-element.12, f32[3,2,1280]{2,0,1:T(4,128)S(1)} %copy.67, ...), kind=kOutput, calls=%fused_computation.6 | convolution fusion | flops 5046927360 | bytes 25088000 | tf_op jit(solution)/shard_map/rsen,snj->rjse/dot_general | solution.py:47
  163.7 10.6 %copy.69 = bf16[3,2560,2,128]{3,2,0,1:T(2,128)(2,1)} copy(bf16[3,2560,2,128]{1,3,0,2:T(8,128)(2,1)} %fusion.7) | data formatting | bytes 7864320 | tf_op jit(solution)/shard_map/convert_element_type | solution.py:49
  174.4 60.6 %all_to_all.36 = bf16[3,2560,2,128]{3,2,0,1:T(2,128)(2,1)S(1)} all-to-all(bf16[3,2560,2,128]{3,2,0,1:T(2,128)(2,1)} %copy.69), channel_id=1, replica_groups=mesh['pole'=2,'wave'=64] {'wave'}, dimensions={1} | all-to-all | bytes 7864320 | tf_op jit(solution)/shard_map/all_to_all | solution.py:50
  235.0 0.5 copy.70
  235.5 0.7 copy.71
  236.2 0.0 copy-start.1
  236.2 2.9 %copy.72 = bf16[3,40,128,128]{3,2,1,0:T(8,128)(2,1)} copy(bf16[3,40,128,128]{3,1,2,0:T(8,128)(2,1)S(1)} %bitcast.66) | data formatting | bytes 7864320 | tf_op jit(solution)/shard_map/all_to_all | solution.py:50
  239.1 0.0 copy-done.1
  (6 shorter events, 0.1 us)
Async XLA Ops:
  6.5 27.1 %copy-start = (f32[32,2]{0,1:T(2,128)S(1)}, f32[32,2]{0,1:T(2,128)}, u32[]{:S(2)}) copy-start(f32[32,2]{0,1:T(2,128)} %param.12) | copy-start | bytes 772
  13.1 12.9 %copy-start.2 = (bf16[32,18,2,1280]{3,2,1,0:T(2,128)(2,1)S(1)}, bf16[32,18,2,1280]{3,2,1,0:T(2,128)(2,1)}, u32[]{:S(2)}) copy-start(bf16[32,18,2,1280]{3,2,1,0:T(2,128)(2,1)} %param.11) | copy-start | bytes 8847364
  13.1 63.2 %all-to-all-start = ((bf16[3,40,128,128]{3,1,0,2:T(8,128)(2,1)}), bf16[3,40,128,128]{3,1,0,2:T(8,128)(2,1)}, u32[]{:S(2)}, u32[]{:S(2)}) async-start(bf16[3,40,128,128]{3,1,0,2:T(8,128)(2,1)} %multiply_convert_fusion), calls=%async_computation | async-start | bytes 7864320 | tf_op jit(solution)/shard_map/all_to_all | solution.py:21
  26.0 63.7 %all-reduce.3.cloned.1.call-start = ((), (), s32[]{:S(2)}) async-start(), calls=%async_computation.3 | async-start | bytes 368640 | tf_op jit(solution)/shard_map/psum | solution.py:41
  29.6 6.5 %copy-start.3 = (s32[2]{0:T(128)S(1)}, s32[2]{0:T(128)}, u32[]{:S(2)}) copy-start(s32[2]{0:T(128)} %param.13) | copy-start | bytes 28
  35.9 112.1 %all-gather.2.cloned.1.call-start = ((), (), s32[]{:S(2)}) async-start(), calls=%async_computation.2 | async-start | bytes 5898240 | tf_op jit(solution)/shard_map/all_gather | solution.py:30
  76.3 2.9 %copy-start.4 = (bf16[3,2,128,1280]{3,2,1,0:T(8,128)(2,1)S(1)}, bf16[3,2,128,1280]{3,2,1,0:T(8,128)(2,1)}, u32[]{:S(2)}) copy-start(bf16[3,2,128,1280]{3,2,1,0:T(8,128)(2,1)} %param.8) | copy-start | bytes 5898244
  236.2 3.0 %copy-start.1 = (f32[32,2]{0,1:T(2,128)S(1)}, f32[32,2]{0,1:T(2,128)}, u32[]{:S(2)}) copy-start(f32[32,2]{0,1:T(2,128)} %param.12) | copy-start | bytes 772
Sparse Core Ops, SparseCore 0:
  36.0 52.8 all-reduce.2
  90.5 57.4 all-gather.1
where the time goes:
time: 247 us; the launch traced here: 246 us
  waiting for transfers between devices  96.7 us (39%)
  blocking collectives  60.6 us (25%)
  local copies, waits for them, and re-layouts  27.4 us (11%)
  matrix products  24 us (10%)
  between operations  13.6 us (6%)
  starting transfers between devices  13.1 us (5%)
  other arithmetic  10.6 us (4%)
    all_to_all x1, blocking collectives, per_device(): lax.all_to_all(synthesized, 'wave', split_axis=1, concat_axis=2, tiled=True)  60.6 us
    all_gather x1, waiting for transfers between devices, per_device(): full_forced = lax.all_gather(forced, 'pole', axis=0, tiled=True)  56.5 us
    all_to_all x1, waiting for transfers between devices, per_device(): lax.all_to_all(weighted, 'wave', split_axis=2, concat_axis=1, tiled=True)  40.1 us
    all_to_all x1, starting transfers between devices, per_device(): lax.all_to_all(weighted, 'wave', split_axis=2, concat_axis=1, tiled=True)  12.9 us
    dot_general x1, matrix products, per_device(): jnp.einsum('rsen,snj->rjse', advanced, legendre, preferred_element_type=j...  12.3 us
    convert_element_type x1, local copies, waits for them, and re-layouts, per_device(): synthesized = jnp.einsum('rsen,snj->rjse', advanced, legendre, preferred_...  10.6 us
    dot_general x1, matrix products, per_device(): jnp.einsum('rjse,snj->rsen', received, legendre, preferred_element_type=j...  10.4 us
    convert_element_type x1, other arithmetic, per_device(): (tendency.astype(jnp.float32) * gauss_weights[None, :, None, None]).astyp...  6.59 us
  transfers between devices with their start and end apart: 3, of which 2 were waited for; matrix products, arithmetic and copies ran while one was open for 10% of the time, Pallas kernels for 0%

commit v1 on v0

v1 whole, which is shorter than its diff:
```python
import jax
import jax.numpy as jnp
from jax import lax
from jax.sharding import PartitionSpec as P

SWAP = [(0, 1), (1, 0)]
EVERY = ("pole", "wave")


def per_device(
    tendency, spectral_state, legendre, gauss_weights, block_inverses, pole_coeffs, wavenumbers
):
    rows, lats, slots, members = tendency.shape
    waves = slots // 2
    degrees = legendre.shape[1]
    pole = lax.axis_index("pole")
    weighted = (tendency.astype(jnp.float32) * gauss_weights[None, :, None, None]).astype(
        jnp.bfloat16
    )
    outgoing = weighted.reshape(rows, lats, waves, 2, members).transpose(3, 2, 0, 1, 4)
    outgoing = outgoing.reshape(2 * waves, rows, lats, members)
    received = lax.all_to_all(outgoing, EVERY, split_axis=0, concat_axis=0, tiled=True)
    received = received.reshape(2, waves, rows, lats, members).transpose(0, 2, 1, 3, 4)
    received = received.reshape(2 * rows, waves * lats, members)

    own_state = lax.dynamic_index_in_dim(spectral_state, pole, 1, keepdims=False)
    other_state = lax.dynamic_index_in_dim(spectral_state, 1 - pole, 1, keepdims=False)
    other_state = lax.ppermute(other_state, "pole", SWAP)
    state = jnp.where(
        pole == 0,
        jnp.concatenate([own_state, other_state], 0),
        jnp.concatenate([other_state, own_state], 0),
    )

    local_pairs = block_inverses.shape[0]
    flat_inverse = block_inverses.reshape(local_pairs, -1).astype(jnp.float32)
    sums = jnp.dot(pole_coeffs.T, flat_inverse, precision=lax.Precision.HIGHEST)
    sums = sums.reshape(2, 2, 3, 3, 2, degrees)
    matrices = jnp.stack([sums[0, 0] - sums[1, 1], sums[0, 1] + sums[1, 0]])
    own_sum = lax.dynamic_index_in_dim(matrices, pole, 3, keepdims=False)
    other_sum = lax.dynamic_index_in_dim(matrices, 1 - pole, 3, keepdims=False)
    matrices = own_sum + lax.ppermute(other_sum, "pole", SWAP)
    real_matrix, imag_matrix = matrices[0], matrices[1]

    table = lax.dynamic_index_in_dim(legendre, pole, 0, keepdims=False)
    wavenumber = lax.dynamic_index_in_dim(wavenumbers, pole, 0, keepdims=False)
    tend = jnp.einsum("rje,nj->ren", received, table, preferred_element_type=jnp.float32)
    live = (lax.broadcasted_iota(jnp.int32, (1, 1, degrees), 2) >= wavenumber).astype(jnp.float32)
    forced = ((state.astype(jnp.float32) + tend) * live).astype(jnp.bfloat16)
    wide = forced.astype(jnp.float32)
    real_rows, imag_rows = [], []
    for row in range(3):
        real = jnp.zeros(wide.shape[1:], jnp.float32)
        imag = jnp.zeros(wide.shape[1:], jnp.float32)
        for column in range(3):
            re, im = real_matrix[row, column][None], imag_matrix[row, column][None]
            real = real + re * wide[column] - im * wide[3 + column]
            imag = imag + re * wide[3 + column] + im * wide[column]
        real_rows.append(real)
        imag_rows.append(imag)
    advanced = jnp.stack(real_rows + imag_rows).astype(jnp.bfloat16)
    grid = jnp.einsum(
        "ren,nj->rje", advanced, table, preferred_element_type=jnp.float32
    ).astype(jnp.bfloat16)
    grid = grid.reshape(2, rows, waves, lats, members).transpose(0, 2, 1, 3, 4)
    grid = grid.reshape(2 * waves, rows, lats, members)
    back = lax.all_to_all(grid, EVERY, split_axis=0, concat_axis=0, tiled=True)
    back = back.reshape(2, waves, rows, lats, members).transpose(2, 3, 1, 0, 4)
    return back.reshape(rows, lats, slots, members)


def solution(mesh):
    in_specs = (
        P("pole", "wave", None, None),
        P("pole", "wave", None, None),
        P("wave", None, None),
        P("wave"),
        P("pole", None, "wave", None),
        P("pole", None),
        P("wave"),
    )
    return jax.shard_map(
        per_device,
        mesh=mesh,
        in_specs=in_specs,
        out_specs=P("pole", "wave", None, None),
        check_vma=False,
    )
```

time: 247 us -> 173 us (0.70)
  waiting for transfers between devices: 96.7 us -> 51.9 us
  between operations: 13.6 us -> 0.25 us
  matrix products: 24 us -> 15.7 us
  local copies, waits for them, and re-layouts: 27.4 us -> 22.4 us
  other arithmetic: 10.6 us -> 7.37 us
    all_gather x1 -> x0, waiting for transfers between devices: 56.5 us -> none  [per_device(): full_forced = lax.all_gather(forced, 'pole', axis=0, tiled=True)]
    ppermute x0 -> x2, waiting for transfers between devices: none -> 51.9 us  [the longest x1 51.9 us: per_device(): matrices = own_sum + lax.ppermute(other_sum, 'pole', SWAP)]
    all_to_all x1, waiting for transfers between devices: 40.1 us -> 0.01 us  [per_device(): lax.all_to_all(outgoing, EVERY, split_axis=0, concat_axis=0, tiled=True)]
    convert_element_type x1 -> x0, local copies, waits for them, and re-layouts: 10.6 us -> none  [per_device(): synthesized = jnp.einsum('rsen,snj->rjse', advanced, legendre, preferred_...]
    dot_general x3, matrix products: 24 us -> 15.7 us  [the longest x1 8.82 us: per_device(): jnp.einsum('rje,nj->ren', received, table, preferred_element_type=jnp.flo...]
    all_to_all x4 -> x0, local copies, waits for them, and re-layouts: 7.05 us -> none  [the longest x3 4.12 us: per_device(): lax.all_to_all(synthesized, 'wave', split_axis=1, concat_axis=2, tiled=True)]
    transpose x0 -> x3, local copies, waits for them, and re-layouts: none -> 6.14 us  [the longest x1 2.87 us: per_device(): received.reshape(2, waves, rows, lats, members).transpose(0, 2, 1, 3, 4)]
    reshape x0 -> x2, local copies, waits for them, and re-layouts: none -> 3.62 us  [the longest x1 2.94 us: per_device(): return back.reshape(rows, lats, slots, members)]
  transfers between devices with their start and end apart: 3 -> 3, of which waited for: 2 -> 1; matrix products, arithmetic and copies ran while one was open for 10% -> 10% of each run, Pallas kernels for 0% -> 0%
where the time goes in v1:
time: 173 us; the launch traced here: 172 us
  blocking collectives  60.9 us (35%)
  waiting for transfers between devices  51.9 us (30%)
  local copies, waits for them, and re-layouts  22.4 us (13%)
  matrix products  15.7 us (9%)
  starting transfers between devices  13.6 us (8%)
  other arithmetic  7.37 us (4%)
    all_to_all x1, blocking collectives, per_device(): back = lax.all_to_all(grid, EVERY, split_axis=0, concat_axis=0, tiled=True)  60.9 us
    ppermute x1, waiting for transfers between devices, per_device(): matrices = own_sum + lax.ppermute(other_sum, 'pole', SWAP)  51.9 us
    all_to_all x1, starting transfers between devices, per_device(): lax.all_to_all(outgoing, EVERY, split_axis=0, concat_axis=0, tiled=True)  11.9 us
    dot_general x1, matrix products, per_device(): jnp.einsum('rje,nj->ren', received, table, preferred_element_type=jnp.flo...  8.82 us
    dot_general x1, matrix products, per_device(): jnp.einsum('ren,nj->rje', advanced, table, preferred_element_type=jnp.flo...  5.61 us
    convert_element_type x1, other arithmetic, per_device(): (tendency.astype(jnp.float32) * gauss_weights[None, :, None, None]).astyp...  4.67 us
    dot_general x1, local copies, waits for them, and re-layouts, per_device(): sums = jnp.dot(pole_coeffs.T, flat_inverse, precision=lax.Precision.HIGHEST)  4.03 us
    reshape x1, local copies, waits for them, and re-layouts, per_device(): flat_inverse = block_inverses.reshape(local_pairs, -1).astype(jnp.float32)  3.47 us
  transfers between devices with their start and end apart: 3, of which 1 were waited for; matrix products, arithmetic and copies ran while one was open for 10% of the time, Pallas kernels for 0%

profile of v1, /device:TPU:1, one launch (start us, length us, event | category | flops | bytes accessed | tf_op | source)
XLA Modules:
  0.0 172.2 jit_solution(7512804652030144285)
XLA Ops:
  0.0 0.0 copy-start
  0.0 4.7 %multiply_convert_fusion = bf16[3,40,128,128]{3,1,2,0:T(8,128)(2,1)S(1)} fusion(bf16[3,40,128,128]{3,2,1,0:T(8,128)(2,1)} %param.7, f32[40]{0:T(128)} %param.10), kind=kLoop, calls=%fused_computation | loop fusion | flops 5898240 | bytes 7864480 | tf_op jit(solution)/shard_map/convert_element_type | solution.py:17
  4.7 2.6 %copy.16 = bf16[2,64,3,40,128]{4,3,2,1,0:T(8,128)(2,1)} copy(bf16[2,64,3,40,128]{4,3,0,1,2:T(8,128)(2,1)S(1)} %bitcast.63) | data formatting | bytes 7864320 | tf_op jit(solution)/shard_map/transpose | solution.py:20
  7.3 11.9 %all-to-all-start = ((bf16[128,3,40,128]{3,2,1,0:T(8,128)(2,1)}), bf16[128,3,40,128]{3,2,1,0:T(8,128)(2,1)}, u32[]{:S(2)}, u32[]{:S(2)}) async-start(bf16[128,3,40,128]{3,2,1,0:T(8,128)(2,1)} %bitcast.59), calls=%async_computation | async-start | bytes 7864320 | tf_op jit(solution)/shard_map/all_to_all | solution.py:22
  19.2 0.0 copy-start.2
  19.2 3.1 %dynamic-slice_bitcast_fusion.1 = (bf16[3,128,1280]{2,1,0:T(8,128)(2,1)}, bf16[3,128,1280]{2,1,0:T(8,128)(2,1)}) fusion(bf16[3,2,128,1280]{3,2,1,0:T(8,128)(2,1)} %param.8, s32[]{:T(128)S(6)} %select_n.22, s32[]{:T(128)S(6)} %select_n.23), kind=kLoop, calls=%fused_computation.14 | loop fusion | bytes 3932168 | tf_op jit(solution)/shard_map/jit(dynamic_index_in_dim)/squeeze | solution.py:26
  22.3 1.4 collective-permute-start.1
  23.7 0.0 copy-done.2
  23.7 3.5 %reshape.307 = bf16[32,46080]{1,0:T(8,128)(2,1)} reshape(bf16[32,18,2,1280]{3,2,1,0:T(2,128)(2,1)S(1)} %copy-done.2) | data formatting | bytes 5898240 | tf_op jit(solution)/shard_map/reshape | solution.py:36
  27.2 0.0 copy-start.4
  27.2 4.0 %dot_general.14 = bf16[2,3,3,2,1280,32]{4,3,2,1,0,5:T(2,128)(2,1)S(1)} reshape(bf16[46080,32]{0,1:T(8,128)(2,1)} %bitcast.64) | data formatting | bytes 5898240 | tf_op jit(solution)/shard_map/dot_general | solution.py:37
  31.2 0.0 copy-done
  31.2 1.3 fusion.9
  32.5 0.2 fusion.23
  32.7 0.1 fusion.19
  32.8 0.4 collective-permute-start
  33.1 0.0 copy-done.4
  33.1 0.6 dynamic_slice.27
  33.8 0.6 fusion.25
  34.4 51.9 %collective-permute-done = f32[2,3,3,1280]{3,0,2,1:T(2,128)S(1)} collective-permute-done((f32[2,3,3,1280]{3,0,2,1:T(2,128)S(1)}, f32[2,3,3,1280]{3,0,2,1:T(2,128)S(1)}, u32[]{:S(2)}, u32[]{:S(2)}) %collective-permute-start) | collective-permute-done | bytes 92192 | tf_op jit(solution)/shard_map/ppermute | solution.py:42
  86.3 0.1 fusion.22
  86.4 0.1 fusion.31
  86.6 0.1 slice_reduce_fusion.4
  86.7 0.1 slice_reduce_fusion.5
  86.8 0.0 all-to-all-done
  86.8 0.0 copy-start.3
  86.8 2.9 %copy.17 = bf16[2,3,64,40,128]{4,3,2,1,0:T(8,128)(2,1)S(1)} copy(bf16[2,3,64,40,128]{4,3,1,2,0:T(8,128)(2,1)} %bitcast.15) | data formatting | bytes 7864320 | tf_op jit(solution)/shard_map/transpose | solution.py:23
  89.7 0.0 collective-permute-done.1
  89.7 0.0 copy-done.3
  89.7 0.0 slice-start
  89.8 0.0 slice-start.1
  89.8 0.0 slice-start.2
  89.8 8.8 %fusion.11 = f32[6,128,1280]{2,1,0:T(8,128)S(1)} fusion(bf16[3,128,1280]{2,1,0:T(8,128)(2,1)} %collective-permute-done.1, bf16[3,128,1280]{2,1,0:T(8,128)(2,1)S(1)} %copy-done.3, f32[1280]{0:T(1024)S(1)} %fusion.25, pred[]{:T(512)S(6)} %eq.3, bf16[6,2560,128]{2,1,0:T(8,128)(2,1)S(1)} %bitcast.65, bf16[2,1280,2560]{2,1,0:T(8,128)(2,1)} %param.9, ...), kind=kOutput, calls=%fused_computation.11 | convolution fusion | flops 5041029120 | bytes 16389125 | tf_op jit(solution)/shard_map/rje,nj->ren/dot_general | solution.py:47
  98.6 0.3 fusion.12
  98.9 0.3 fusion.13
  99.2 0.0 slice-start.3
  99.2 0.3 fusion.14
  99.5 0.3 fusion.15
  99.7 0.3 fusion.16
  100.0 0.3 fusion.17
  100.3 0.0 slice-done
  100.3 0.0 slice-done.1
  100.3 0.0 slice-done.2
  100.3 1.0 slice-done.3
  101.4 5.6 %fusion.6 = bf16[2560,6,128]{2,0,1:T(8,128)(2,1)S(1)} fusion(bf16[6,128,1280]{2,1,0:T(8,128)(2,1)S(1)} %fusion.17, bf16[2,1280,2560]{2,1,0:T(8,128)(2,1)S(1)} %bitcast.68, s32[]{:T(128)S(6)} %select_n.22), kind=kOutput, calls=%fused_computation.7 | convolution fusion | flops 5035130880 | bytes 12451844 | tf_op jit(solution)/shard_map/ren,nj->rje/dot_general | solution.py:62
  107.0 0.7 copy.20
  107.7 60.9 %all_to_all.10 = bf16[128,3,40,128]{3,2,1,0:T(8,128)(2,1)S(1)} all-to-all(bf16[128,3,40,128]{3,2,1,0:T(8,128)(2,1)S(1)} %bitcast.60), channel_id=1, replica_groups=mesh['pole'=2,'wave'=64] {'pole','wave'}, dimensions={0} | all-to-all | bytes 7864320 | tf_op jit(solution)/shard_map/all_to_all | solution.py:67
  168.6 0.7 copy.21
  169.2 0.0 copy-start.1
  169.2 2.9 %copy.22 = bf16[3,40,128,128]{3,2,1,0:T(8,128)(2,1)} copy(bf16[3,40,128,128]{3,1,2,0:T(8,128)(2,1)S(1)} %bitcast.62) | data formatting | bytes 7864320 | tf_op jit(solution)/shard_map/reshape | solution.py:69
  172.2 0.0 copy-done.1
  (2 shorter events, 0.0 us)
Async XLA Ops:
  0.0 31.2 %copy-start = (f32[32,2]{0,1:T(2,128)S(1)}, f32[32,2]{0,1:T(2,128)}, u32[]{:S(2)}) copy-start(f32[32,2]{0,1:T(2,128)} %param.12) | copy-start | bytes 772
  7.3 79.6 %all-to-all-start = ((bf16[128,3,40,128]{3,2,1,0:T(8,128)(2,1)}), bf16[128,3,40,128]{3,2,1,0:T(8,128)(2,1)}, u32[]{:S(2)}, u32[]{:S(2)}) async-start(bf16[128,3,40,128]{3,2,1,0:T(8,128)(2,1)} %bitcast.59), calls=%async_computation | async-start | bytes 7864320 | tf_op jit(solution)/shard_map/all_to_all | solution.py:22
  19.2 4.5 %copy-start.2 = (bf16[32,18,2,1280]{3,2,1,0:T(2,128)(2,1)S(1)}, bf16[32,18,2,1280]{3,2,1,0:T(2,128)(2,1)}, u32[]{:S(2)}) copy-start(bf16[32,18,2,1280]{3,2,1,0:T(2,128)(2,1)} %param.11) | copy-start | bytes 8847364
  22.3 67.4 %collective-permute-start.1 = (bf16[3,128,1280]{2,1,0:T(8,128)(2,1)}, bf16[3,128,1280]{2,1,0:T(8,128)(2,1)}, u32[]{:S(2)}, u32[]{:S(2)}) collective-permute-start(bf16[3,128,1280]{2,1,0:T(8,128)(2,1)} %get-tuple-element.24), channel_id=1, source_target_pairs={{0,64},{64,0},{1,65},{65,1},{2,66},{66,2},{3,67},{67,3},{4,68},{68... | collective-permute-start | bytes 2949128 | tf_op jit(solution)/shard_map/ppermute | solution.py:28
  27.2 6.0 %copy-start.4 = (s32[2]{0:T(128)S(1)}, s32[2]{0:T(128)}, u32[]{:S(2)}) copy-start(s32[2]{0:T(128)} %param.13) | copy-start | bytes 28
  32.8 53.6 %collective-permute-start = (f32[2,3,3,1280]{3,0,2,1:T(2,128)S(1)}, f32[2,3,3,1280]{3,0,2,1:T(2,128)S(1)}, u32[]{:S(2)}, u32[]{:S(2)}) collective-permute-start(f32[2,3,3,1280]{3,0,2,1:T(2,128)S(1)} %fusion.19), channel_id=1, source_target_pairs={{0,64},{64,0},{1,65},{65,1},{2,66},{66,2},{3,67},{67,3},{4,68},{68... | collective-permute-start | bytes 276488 | tf_op jit(solution)/shard_map/ppermute | solution.py:42
  86.8 2.9 %copy-start.3 = (bf16[3,128,1280]{2,1,0:T(8,128)(2,1)S(1)}, bf16[3,128,1280]{2,1,0:T(8,128)(2,1)}, u32[]{:S(2)}) copy-start(bf16[3,128,1280]{2,1,0:T(8,128)(2,1)} %get-tuple-element.23) | copy-start | bytes 2949124
  89.7 10.6 %slice-start = ((s8[13107200]{0:T(1024)(128)(4,1)}), s8[524288]{0:T(1024)(128)(4,1)S(1)}, s32[]{:S(2)}) async-start(s8[13107200]{0:T(1024)(128)(4,1)} %bitcast.67), calls=%async_computation.2 | async-start | bytes 1048576
  89.8 10.6 %slice-start.1 = ((s8[13107200]{0:T(1024)(128)(4,1)}), s8[4194304]{0:T(1024)(128)(4,1)S(1)}, s32[]{:S(2)}) async-start(s8[13107200]{0:T(1024)(128)(4,1)} %bitcast.67), calls=%async_computation.3 | async-start | bytes 8388608
  89.8 10.6 %slice-start.2 = ((s8[13107200]{0:T(1024)(128)(4,1)}), s8[4194304]{0:T(1024)(128)(4,1)S(1)}, s32[]{:S(2)}) async-start(s8[13107200]{0:T(1024)(128)(4,1)} %bitcast.67), calls=%async_computation.4 | async-start | bytes 8388608
  99.2 2.2 %slice-start.3 = ((s8[13107200]{0:T(1024)(128)(4,1)}), s8[4194304]{0:T(1024)(128)(4,1)S(1)}, s32[]{:S(2)}) async-start(s8[13107200]{0:T(1024)(128)(4,1)} %bitcast.67), calls=%async_computation.5 | async-start | bytes 8388608
  169.2 3.0 %copy-start.1 = (f32[32,2]{0,1:T(2,128)S(1)}, f32[32,2]{0,1:T(2,128)}, u32[]{:S(2)}) copy-start(f32[32,2]{0,1:T(2,128)} %param.12) | copy-start | bytes 772
